TPU v7x, 256 devices: a whole 4x4x8 slice. The times are simulated.
256 devices in a mesh: view: 4 (over y_hi, core), row: 8 (over z), col: 8 (over y_lo, x).
Axes of the slice: x: 4, y: 4 (y_hi: 2, y_lo: 2; y = y_hi * 2 + y_lo), z: 8, core: 2. Of those that a mesh axis runs over, the one named last changes fastest.
Arguments:
- view_maps: bfloat16 [16, 32, 128, 768], P('view', 'row', 'col'), may hold values from -6 to 6
- gain_spatial: float32 [768], replicated, may hold values from 0.1 to 1.9
- spatial_query: bfloat16 [768, 768], replicated, may hold values from -8 to 8
- spatial_key: bfloat16 [768, 768], replicated, may hold values from -8 to 8
- spatial_value: bfloat16 [768, 768], replicated, may hold values from -0.21875 to 0.21875
- spatial_output: bfloat16 [768, 768], replicated, may hold values from -0.21875 to 0.21875
- gain_temporal: float32 [768], replicated, may hold values from 0.1 to 1.9
- temporal_query: bfloat16 [768, 768], replicated, may hold values from -8 to 8
- temporal_key: bfloat16 [768, 768], replicated, may hold values from -8 to 8
- temporal_value: bfloat16 [768, 768], replicated, may hold values from -0.21875 to 0.21875
- temporal_output: bfloat16 [768, 768], replicated, may hold values from -0.21875 to 0.21875
Outputs:
- refined: bfloat16 [16, 32, 128, 768], P('view', 'row', 'col')
All inputs are finite; a program needn't handle non-finite values.
Results may differ from a plain program's by a relative error of at most 0.012.
Values may be sent and summed in bfloat16 or wider, within the bound.
No kernel may reach another device: no remote copies, remote signals or barrier semaphores. Data moves between devices by JAX's collectives and lax.ppermute only.
A program may use at most 64 MiB of HBM per device.

v0:
```python
import jax
import jax.numpy as jnp
from jax import lax
from jax.sharding import PartitionSpec as P

HEADS = 12
HEAD_DIM = 64
RADIUS = 3
epsilon = 1e-06
very_negative = -1e30


def padded(block, sides, width):
    for axis, dim in sides:
        count = lax.axis_size(axis)
        forward = [(i, i + 1) for i in range(count - 1)]
        backward = [(target, source) for source, target in forward]
        low = lax.ppermute(
            lax.slice_in_dim(block, block.shape[dim] - width, None, axis=dim), axis, forward
        )
        high = lax.ppermute(lax.slice_in_dim(block, 0, width, axis=dim), axis, backward)
        block = jnp.concatenate([low, block, high], axis=dim)
    return block


def rms_norm(tokens, gain_vector):
    values = tokens.astype(jnp.float32)
    scaled = values * lax.rsqrt(jnp.mean(values * values, axis=-1, keepdims=True) + epsilon)
    return (scaled * gain_vector).astype(jnp.bfloat16)


def project(tokens, weight_matrix):
    flat = tokens.reshape(-1, tokens.shape[-1])
    result = jnp.dot(flat, weight_matrix, preferred_element_type=jnp.float32)
    return result.reshape(tokens.shape[:-1] + (weight_matrix.shape[1],))


def grid_rows(count_rows, count_cols):
    return jnp.broadcast_to(
        jnp.arange(count_rows, dtype=jnp.int32)[:, None], (count_rows, count_cols)
    ).reshape(-1)


def grid_cols(count_rows, count_cols):
    return jnp.broadcast_to(
        jnp.arange(count_cols, dtype=jnp.int32)[None, :], (count_rows, count_cols)
    ).reshape(-1)


def neighbour(queries, keys_wide, values_wide, first_row, first_col, total_rows, total_cols):
    local_views, height, width, features = queries.shape
    wide_rows, wide_cols = (keys_wide.shape[1], keys_wide.shape[2])
    factor = HEAD_DIM ** (-0.5)
    query_rows = grid_rows(height, width)
    query_cols = grid_cols(height, width)
    key_rows = grid_rows(wide_rows, wide_cols)
    key_cols = grid_cols(wide_rows, wide_cols)
    row_gap = key_rows[None, :] - RADIUS - query_rows[:, None]
    col_gap = key_cols[None, :] - RADIUS - query_cols[:, None]
    in_band = (jnp.abs(row_gap) <= RADIUS) & (jnp.abs(col_gap) <= RADIUS)
    global_rows = first_row - RADIUS + key_rows
    global_cols = first_col - RADIUS + key_cols
    inside = (
        (global_rows >= 0)
        & (global_rows < total_rows)
        & (global_cols >= 0)
        & (global_cols < total_cols)
    )
    allowed = (in_band & inside[None, :])[None, :, :]

    def one_view(items):
        query_heads = items[0].reshape(height * width, HEADS, HEAD_DIM)
        key_heads = items[1].reshape(wide_rows * wide_cols, HEADS, HEAD_DIM)
        value_heads = items[2].reshape(wide_rows * wide_cols, HEADS, HEAD_DIM).astype(jnp.float32)
        scores = (
            jnp.einsum("qhe,khe->hqk", query_heads, key_heads, preferred_element_type=jnp.float32)
            * factor
        )
        scores = jnp.where(allowed, scores, very_negative)
        highest = jnp.max(scores, axis=-1, keepdims=True)
        weights = jnp.exp(scores - highest)
        weights = weights / jnp.sum(weights, axis=-1, keepdims=True)
        mixed = jnp.einsum("hqk,khe->qhe", weights, value_heads, precision=lax.Precision.HIGHEST)
        return mixed.reshape(height, width, features).astype(jnp.bfloat16)

    return lax.map(one_view, (queries, keys_wide, values_wide))


def body(
    view_maps,
    gain_spatial,
    spatial_query,
    spatial_key,
    spatial_value,
    spatial_output,
    gain_temporal,
    temporal_query,
    temporal_key,
    temporal_value,
    temporal_output,
):
    local_views, tile_rows, tile_cols = (view_maps.shape[0], view_maps.shape[1], view_maps.shape[2])
    total_rows = lax.axis_size("row") * tile_rows
    total_cols = lax.axis_size("col") * tile_cols
    first_row = lax.axis_index("row") * tile_rows
    first_col = lax.axis_index("col") * tile_cols
    normed = rms_norm(view_maps, gain_spatial)
    queries = project(normed, spatial_query).astype(jnp.bfloat16)
    keys = project(normed, spatial_key).astype(jnp.bfloat16)
    values = project(normed, spatial_value).astype(jnp.bfloat16)
    stacked = jnp.stack([keys, values], 0)
    widened = padded(stacked, (("row", 2), ("col", 3)), RADIUS)
    keys_wide = widened[0]
    values_wide = widened[1]
    attended = neighbour(
        queries, keys_wide, values_wide, first_row, first_col, total_rows, total_cols
    )
    middle = (view_maps.astype(jnp.float32) + project(attended, spatial_output)).astype(
        jnp.bfloat16
    )
    normed_time = rms_norm(middle, gain_temporal)
    factor = HEAD_DIM ** (-0.5)
    positions = tile_rows * tile_cols
    query_time = project(normed_time, temporal_query).astype(jnp.bfloat16)
    key_time = project(normed_time, temporal_key).astype(jnp.bfloat16)
    value_time = project(normed_time, temporal_value).astype(jnp.bfloat16)
    query_heads = query_time.reshape(local_views, positions, HEADS, HEAD_DIM)
    running_max = jnp.full((local_views, positions, HEADS), very_negative, jnp.float32)
    key_heads = lax.all_gather(key_time, "view", axis=0, tiled=True).reshape(
        -1, positions, HEADS, HEAD_DIM
    )
    value_heads = (
        lax.all_gather(value_time, "view", axis=0, tiled=True)
        .reshape(-1, positions, HEADS, HEAD_DIM)
        .astype(jnp.float32)
    )
    scores = (
        jnp.einsum("qphe,kphe->qkph", query_heads, key_heads, preferred_element_type=jnp.float32)
        * factor
    )
    new_max = jnp.maximum(running_max, jnp.max(scores, axis=1))
    weights = jnp.exp(scores - new_max[:, None])
    new_sum = jnp.sum(weights, axis=1)
    new_acc = jnp.einsum("qkph,kphe->qphe", weights, value_heads)
    attended_time = (new_acc / new_sum[..., None]).reshape(view_maps.shape).astype(jnp.bfloat16)
    refined = (middle.astype(jnp.float32) + project(attended_time, temporal_output)).astype(
        jnp.bfloat16
    )
    return refined


def solution(mesh):
    return jax.shard_map(
        body,
        mesh=mesh,
        in_specs=(P("view", "row", "col", None), P(), P(), P(), P(), P(), P(), P(), P(), P(), P()),
        out_specs=P("view", "row", "col", None),
        check_vma=False,
    )
```

profile of v0, /device:TPU:1, one launch (start us, length us, event | category | flops | bytes accessed | tf_op | source)
XLA Modules:
  0.0 165.9 jit_solution(17304333860771478719)
XLA Ops:
  6.6 1.3 fusion.40
  7.9 1.9 %fusion.28 = bf16[1,4,4,16,768]{4,3,2,1,0:T(8,128)(2,1)S(1)} fusion(bf16[768,768]{1,0:T(8,128)(2,1)} %param.16, bf16[4,4,16,768]{3,2,1,0:T(8,128)(2,1)} %param.13, f32[768]{0:T(1024)} %param.14, f32[4,4,16]{2,1,0:T(4,128)S(1)} %add_rsqrt_fusion.1), kind=kOutput, calls=%fused_computation.46 | convolution fusion | flops 302972928 | bytes 1970176 | tf_op jit(solution)/shard_map/dot_general | solution.py:34
  10.4 1.1 fusion.45
  11.5 4.4 %collective-permute-start = (bf16[2,4,3,16,768]{4,3,2,1,0:T(8,128)(2,1)}, bf16[2,4,3,16,768]{4,3,2,1,0:T(8,128)(2,1)S(1)}, u32[]{:S(2)}, u32[]{:S(2)}) collective-permute-start(bf16[2,4,3,16,768]{4,3,2,1,0:T(8,128)(2,1)} %get-tuple-element.103), channel_id=1, source_target_pairs={{0,8},{8,16},{16,24},{24,32},{32,40},{40,48},{48,56},{1,9},{9,17},... | collective-permute-start | bytes 1769480 | tf_op jit(solution)/shard_map/ppermute | solution.py:18
  15.9 1.3 collective-permute-start.1
  18.0 10.2 %collective-permute-done = bf16[2,4,3,16,768]{4,3,2,1,0:T(8,128)(2,1)S(1)} collective-permute-done((bf16[2,4,3,16,768]{4,3,2,1,0:T(8,128)(2,1)}, bf16[2,4,3,16,768]{4,3,2,1,0:T(8,128)(2,1)S(1)}, u32[]{:S(2)}, u32[]{:S(2)}) %collective-permute-start) | collective-permute-done | bytes 589856 | tf_op jit(solution)/shard_map/ppermute | solution.py:18
  28.2 4.1 %collective-permute-done.1 = bf16[2,4,3,16,768]{4,3,2,1,0:T(8,128)(2,1)S(1)} collective-permute-done((bf16[2,4,3,16,768]{4,3,2,1,0:T(8,128)(2,1)}, bf16[2,4,3,16,768]{4,3,2,1,0:T(8,128)(2,1)S(1)}, u32[]{:S(2)}, u32[]{:S(2)}) %collective-permute-start.1) | collective-permute-done | bytes 589856 | tf_op jit(solution)/shard_map/ppermute | solution.py:21
  32.2 1.3 pad_maximum_fusion.5
  33.6 3.9 %collective-permute-start.2 = (bf16[2,4,10,3,768]{4,3,2,1,0:T(4,128)(2,1)}, bf16[2,4,10,3,768]{4,3,2,1,0:T(4,128)(2,1)}, u32[]{:S(2)}, u32[]{:S(2)}) collective-permute-start(bf16[2,4,10,3,768]{4,3,2,1,0:T(4,128)(2,1)} %get-tuple-element.101), channel_id=1, source_target_pairs={{0,1},{1,2},{2,3},{3,4},{4,5},{5,6},{6,7},{8,9},{9,10},{10,11},{11... | collective-permute-start | bytes 1105928 | tf_op jit(solution)/shard_map/ppermute | solution.py:18
  37.5 1.3 collective-permute-start.3
  39.5 0.7 sub.85
  40.3 2.6 %convolution_convert_fusion.4 = bf16[4,4,16,768]{3,2,1,0:T(8,128)(2,1)} fusion(bf16[768,768]{1,0:T(8,128)(2,1)} %param.15, bf16[4,4,16,768]{3,2,1,0:T(8,128)(2,1)S(1)} %copy-done.2, f32[768]{0:T(1024)} %param.14, f32[4,4,16]{2,1,0:T(4,128)} %copy-done.4), kind=kOutput, calls=%fused_computation.43 | convolution fusion | flops 302972928 | bytes 1970176 | tf_op jit(solution)/shard_map/dot_general | solution.py:34
  42.8 3.1 %collective-permute-done.2 = bf16[2,4,10,3,768]{4,3,2,1,0:T(4,128)(2,1)} collective-permute-done((bf16[2,4,10,3,768]{4,3,2,1,0:T(4,128)(2,1)}, bf16[2,4,10,3,768]{4,3,2,1,0:T(4,128)(2,1)}, u32[]{:S(2)}, u32[]{:S(2)}) %collective-permute-start.2) | collective-permute-done | bytes 368672 | tf_op jit(solution)/shard_map/ppermute | solution.py:18
  45.9 4.6 %collective-permute-done.3 = bf16[2,4,10,3,768]{4,3,2,1,0:T(4,128)(2,1)} collective-permute-done((bf16[2,4,10,3,768]{4,3,2,1,0:T(4,128)(2,1)}, bf16[2,4,10,3,768]{4,3,2,1,0:T(4,128)(2,1)}, u32[]{:S(2)}, u32[]{:S(2)}) %collective-permute-start.3) | collective-permute-done | bytes 368672 | tf_op jit(solution)/shard_map/ppermute | solution.py:21
  50.5 3.1 %pad_maximum_fusion = bf16[2,4,10,22,768]{4,3,2,1,0:T(8,128)(2,1)S(1)} fusion(bf16[2,4,10,3,768]{4,3,2,1,0:T(4,128)(2,1)} %collective-permute-done.3, bf16[2,4,3,16,768]{4,3,2,1,0:T(8,128)(2,1)S(1)} %collective-permute-done.1, bf16[1,4,4,16,768]{4,3,2,1,0:T(8,128)(2,1)S(1)} %fusion.29, bf16[1,4,4,16,768]{4,3,2,1,0:T(8,128)(2,1)S(1)} %fusion.28, ...), kind=kLoop, calls=%fused_computation.26 | loop fusion | flops 16220160 | bytes 5406720 | tf_op jit(solution)/shard_map/concatenate | solution.py:22
  53.6 1.8 %slice_bitcast_fusion = (bf16[4,10,22,768]{3,2,1,0:T(8,128)(2,1)}, bf16[4,10,22,768]{3,2,1,0:T(8,128)(2,1)}) fusion(bf16[2,4,10,22,768]{4,3,2,1,0:T(8,128)(2,1)S(1)} %pad_maximum_fusion), kind=kLoop, calls=%fused_computation.33 | loop fusion | bytes 5406720 | tf_op jit(solution)/shard_map/squeeze | solution.py:113
  55.4 26.6 %while.11 = (s32[]{:T(128)}, bf16[4,4,16,768]{3,2,1,0:T(8,128)(2,1)}, bf16[4,10,22,768]{3,2,1,0:T(8,128)(2,1)}, bf16[4,4,16,768]{3,2,1,0:T(8,128)(2,1)}, bf16[4,...) while((s32[]{:T(128)}, ...), condition=%wide.region_4.5_spmd.clone, body=%wide.region_1.4_spmd.clone.sunk | while | flops 152731136 | bytes 6633009 | solution.py:86
  55.4 1.1 constant_dynamic-slice_fusion.5
  57.2 0.9 constant_dynamic-slice_fusion.6
  59.9 1.2 fusion.73
  61.4 0.7 constant_dynamic-update-slice_fusion.2
  62.1 1.1 constant_dynamic-slice_fusion.5
  63.9 0.9 constant_dynamic-slice_fusion.6
  66.5 1.2 fusion.73
  68.1 0.7 constant_dynamic-update-slice_fusion.2
  68.8 1.1 constant_dynamic-slice_fusion.5
  70.6 0.9 constant_dynamic-slice_fusion.6
  71.6 0.6 fusion.71
  73.2 1.2 fusion.73
  74.8 0.7 constant_dynamic-update-slice_fusion.2
  75.4 1.1 constant_dynamic-slice_fusion.5
  77.2 0.9 constant_dynamic-slice_fusion.6
  78.3 0.6 fusion.71
  79.8 1.2 fusion.73
  81.4 0.7 constant_dynamic-update-slice_fusion.2
  82.1 1.8 %multiply_reduce_fusion = (f32[4,4,16]{2,1,0:T(4,128)S(1)}, f32[4,4,16,768]{3,2,1,0:T(8,128)S(1)}) fusion(bf16[4,4,16,768]{3,2,1,0:T(8,128)(2,1)} %get-tuple-element.37, bf16[768,768]{1,0:T(8,128)(2,1)S(1)} %copy-done, bf16[4,4,16,768]{3,2,1,0:T(8,128)(2,1)} %param.13), kind=kOutput, calls=%fused_computation.67 | convolution fusion | flops 303169280 | bytes 2753536 | tf_op jit(solution)/shard_map/dot_general | solution.py:34
  84.0 1.2 convolution_convert_fusion.2
  85.5 1.2 convolution_convert_fusion.3
  86.8 1.7 %convolution_convert_fusion.1 = bf16[4,4,16,768]{3,2,1,0:T(8,128)(2,1)S(1)} fusion(bf16[4,4,16,768]{3,2,1,0:T(8,128)(2,1)S(1)} %multiply_convert_fusion, bf16[768,768]{1,0:T(8,128)(2,1)} %param.20), kind=kOutput, calls=%fused_computation.40 | convolution fusion | flops 302186496 | bytes 1966080 | tf_op jit(solution)/shard_map/dot_general | solution.py:34
  89.2 28.3 %all-gather.5.cloned.1.call-done = bf16[16,4,16,768]{3,2,1,0:T(8,128)(2,1)} async-done(((bf16[4,4,16,768]{3,2,1,0:T(8,128)(2,1)}), bf16[16,4,16,768]{3,2,1,0:T(8,128)(2,1)}) %all-gather.5.cloned.1.call-update) | async-done | bytes 1572880 | tf_op jit(solution)/shard_map/all_gather | solution.py:129
  117.5 5.9 %reshape.289 = bf16[16,64,12,64]{3,2,1,0:T(8,128)(2,1)} reshape(bf16[16,4,16,768]{3,2,1,0:T(8,128)(2,1)} %all-gather.5.cloned.1.call-done) | data formatting | bytes 3145728 | tf_op jit(solution)/shard_map/reshape | solution.py:129
  123.4 5.0 %bitcast_reduce_fusion = (f32[4,64,12]{0,2,1:T(8,128)S(1)}, f32[64,12,16,4]{2,3,1,0:T(4,128)S(1)}) fusion(bf16[4,64,12,64]{3,2,1,0:T(8,128)(2,1)S(1)} %reshape.290, bf16[16,64,12,64]{3,2,1,0:T(8,128)(2,1)} %reshape.289), kind=kOutput, calls=%fused_computation.29 | convolution fusion | flops 6386688 | bytes 2174976 | tf_op jit(solution)/shard_map/qphe,kphe->qkph/dot_general | solution.py:138
  128.4 1.1 copy-done.1
  129.5 1.9 %fusion.30 = f32[4,64,12]{0,2,1:T(8,128)S(1)} fusion(f32[64,12,16,4]{2,3,1,0:T(4,128)S(1)} %get-tuple-element.108, f32[4,64,12]{0,2,1:T(8,128)S(1)} %broadcast_maximum_fusion), kind=kLoop, calls=%fused_computation.48 | loop fusion | flops 95232 | bytes 221184 | tf_op jit(solution)/shard_map/reduce_sum | solution.py:143
  131.4 13.6 %all-gather.3.cloned.1.call-done = bf16[16,4,16,768]{3,2,1,0:T(8,128)(2,1)} async-done(((bf16[4,4,16,768]{3,2,1,0:T(8,128)(2,1)}), bf16[16,4,16,768]{3,2,1,0:T(8,128)(2,1)}) %all-gather.3.cloned.1.call-update) | async-done | bytes 1572880 | tf_op jit(solution)/shard_map/all_gather | solution.py:133
  145.0 5.9 %reshape.288 = bf16[16,64,12,64]{3,2,1,0:T(8,128)(2,1)} reshape(bf16[16,4,16,768]{3,2,1,0:T(8,128)(2,1)} %all-gather.3.cloned.1.call-done) | data formatting | bytes 3145728 | tf_op jit(solution)/shard_map/reshape | solution.py:134
  150.9 4.9 %fusion.19 = bf16[4,64,12,64]{3,0,2,1:T(4,128)(2,1)S(1)} fusion(bf16[16,64,12,64]{3,2,1,0:T(8,128)(2,1)} %reshape.288, f32[64,12,16,4]{2,3,1,0:T(4,128)} %copy-done.1, f32[4,64,12]{0,2,1:T(8,128)S(1)} %fusion.30, f32[4,64,12]{0,2,1:T(8,128)S(1)} %broadcast_maximum_fusion), kind=kOutput, calls=%fused_computation.31 | convolution fusion | flops 6733824 | bytes 2187264 | tf_op jit(solution)/shard_map/qkph,kphe->qphe/dot_general | solution.py:144
  156.6 2.5 %fusion.27 = bf16[4,4,16,768]{3,2,1,0:T(8,128)(2,1)} fusion(f32[4,4,16,768]{3,2,1,0:T(8,128)S(1)} %get-tuple-element.106, bf16[4,4,16,768]{3,2,1,0:T(8,128)(2,1)S(1)} %convert_element_type.76, bf16[768,768]{1,0:T(8,128)(2,1)} %param.23), kind=kOutput, calls=%fused_computation.39 | convolution fusion | flops 302383104 | bytes 2752512 | tf_op jit(solution)/shard_map/dot_general | solution.py:34
  (71 shorter events, 13.6 us)
Async XLA Ops:
  6.5 75.5 %copy-start = (bf16[768,768]{1,0:T(8,128)(2,1)S(1)}, bf16[768,768]{1,0:T(8,128)(2,1)}, u32[]{:S(2)}) copy-start(bf16[768,768]{1,0:T(8,128)(2,1)} %param.18) | copy-start | bytes 3538948
  6.5 3.3 %copy-start.2 = (bf16[4,4,16,768]{3,2,1,0:T(8,128)(2,1)S(1)}, bf16[4,4,16,768]{3,2,1,0:T(8,128)(2,1)}, u32[]{:S(2)}) copy-start(bf16[4,4,16,768]{3,2,1,0:T(8,128)(2,1)} %param.13) | copy-start | bytes 1179652
  6.5 3.3 %copy-start.9 = (f32[768]{0:T(1024)S(1)}, f32[768]{0:T(1024)}, u32[]{:S(2)}) copy-start(f32[768]{0:T(1024)} %param.14) | copy-start | bytes 9220
  6.5 111.0 %all-gather.5.cloned.1.call-start = ((), (), s32[]{:S(2)}) async-start(), calls=%async_computation.1 | async-start | bytes 1966080 | tf_op jit(solution)/shard_map/all_gather | solution.py:129
  6.5 3.3 %copy-start.6 = (bf16[768,768]{1,0:T(8,128)(2,1)S(1)}, bf16[768,768]{1,0:T(8,128)(2,1)}, u32[]{:S(2)}) copy-start(bf16[768,768]{1,0:T(8,128)(2,1)} %param.17) | copy-start | bytes 3538948
  7.9 2.5 %copy-start.4 = (f32[4,4,16]{2,1,0:T(4,128)}, f32[4,4,16]{2,1,0:T(4,128)S(1)}, u32[]{:S(2)}) copy-start(f32[4,4,16]{2,1,0:T(4,128)S(1)} %add_rsqrt_fusion.1) | copy-start | bytes 3076
  11.5 16.7 %collective-permute-start = (bf16[2,4,3,16,768]{4,3,2,1,0:T(8,128)(2,1)}, bf16[2,4,3,16,768]{4,3,2,1,0:T(8,128)(2,1)S(1)}, u32[]{:S(2)}, u32[]{:S(2)}) collective-permute-start(bf16[2,4,3,16,768]{4,3,2,1,0:T(8,128)(2,1)} %get-tuple-element.103), channel_id=1, source_target_pairs={{0,8},{8,16},{16,24},{24,32},{32,40},{40,48},{48,56},{1,9},{9,17},... | collective-permute-start | bytes 1769480 | tf_op jit(solution)/shard_map/ppermute | solution.py:18
  15.9 16.3 %collective-permute-start.1 = (bf16[2,4,3,16,768]{4,3,2,1,0:T(8,128)(2,1)}, bf16[2,4,3,16,768]{4,3,2,1,0:T(8,128)(2,1)S(1)}, u32[]{:S(2)}, u32[]{:S(2)}) collective-permute-start(bf16[2,4,3,16,768]{4,3,2,1,0:T(8,128)(2,1)} %get-tuple-element.104), channel_id=1, source_target_pairs={{8,0},{16,8},{24,16},{32,24},{40,32},{48,40},{56,48},{9,1},{17,9},... | collective-permute-start | bytes 1769480 | tf_op jit(solution)/shard_map/ppermute | solution.py:21
  33.6 12.3 %collective-permute-start.2 = (bf16[2,4,10,3,768]{4,3,2,1,0:T(4,128)(2,1)}, bf16[2,4,10,3,768]{4,3,2,1,0:T(4,128)(2,1)}, u32[]{:S(2)}, u32[]{:S(2)}) collective-permute-start(bf16[2,4,10,3,768]{4,3,2,1,0:T(4,128)(2,1)} %get-tuple-element.101), channel_id=1, source_target_pairs={{0,1},{1,2},{2,3},{3,4},{4,5},{5,6},{6,7},{8,9},{9,10},{10,11},{11... | collective-permute-start | bytes 1105928 | tf_op jit(solution)/shard_map/ppermute | solution.py:18
  37.5 13.0 %collective-permute-start.3 = (bf16[2,4,10,3,768]{4,3,2,1,0:T(4,128)(2,1)}, bf16[2,4,10,3,768]{4,3,2,1,0:T(4,128)(2,1)}, u32[]{:S(2)}, u32[]{:S(2)}) collective-permute-start(bf16[2,4,10,3,768]{4,3,2,1,0:T(4,128)(2,1)} %get-tuple-element.102), channel_id=1, source_target_pairs={{1,0},{2,1},{3,2},{4,3},{5,4},{6,5},{7,6},{9,8},{10,9},{11,10},{12... | collective-permute-start | bytes 1105928 | tf_op jit(solution)/shard_map/ppermute | solution.py:21
  53.6 1.8 %copy-start.3 = (pred[220]{0:T(512)(128)(4,1)S(1)}, pred[220]{0:T(512)(128)(4,1)}, u32[]{:S(2)}) copy-start(pred[220]{0:T(512)(128)(4,1)} %reshape.291) | copy-start | bytes 664
  82.1 1.8 %copy-start.5 = (f32[768]{0:T(1024)S(1)}, f32[768]{0:T(1024)}, u32[]{:S(2)}) copy-start(f32[768]{0:T(1024)} %param.19) | copy-start | bytes 9220
  82.1 1.9 %copy-start.7 = (bf16[768,768]{1,0:T(8,128)(2,1)S(1)}, bf16[768,768]{1,0:T(8,128)(2,1)}, u32[]{:S(2)}) copy-start(bf16[768,768]{1,0:T(8,128)(2,1)} %param.21) | copy-start | bytes 3538948
  84.0 1.5 copy-start.8
  85.3 59.7 %all-gather.3.cloned.1.call-start = ((), (), s32[]{:S(2)}) async-start(), calls=%async_computation | async-start | bytes 1966080 | tf_op jit(solution)/shard_map/all_gather | solution.py:133
  128.4 1.2 copy-start.1
Sparse Core Ops, SparseCore 0:
  85.4 32.0 all-gather.4
  119.3 25.6 all-gather.2
where the time goes:
time: 167 us; the launch traced here: 166 us
  waiting for transfers between devices  63.9 us (38%)
  local copies, waits for them, and re-layouts  35.8 us (21%)
  matrix products  30.5 us (18%)
  between operations  13.7 us (8%)
  starting transfers between devices  11.1 us (7%)
  other arithmetic  10.8 us (6%)
    all_gather x1, waiting for transfers between devices, body(): lax.all_gather(key_time, 'view', axis=0, tiled=True)  28.3 us
    all_gather x1, waiting for transfers between devices, body(): lax.all_gather(value_time, 'view', axis=0, tiled=True)  13.6 us
    dot_general x8, matrix products, project(): result = jnp.dot(flat, weight_matrix, preferred_element_type=jnp.float32)  13.5 us
    ppermute x2, waiting for transfers between devices, padded(): lax.ppermute(lax.slice_in_dim(block, block.shape[dim] - width, None, axis...  13.3 us
    ppermute x2, waiting for transfers between devices, padded(): lax.ppermute(lax.slice_in_dim(block, 0, width, axis=dim), axis, backward)  8.65 us
    ppermute x2, starting transfers between devices, padded(): lax.ppermute(lax.slice_in_dim(block, block.shape[dim] - width, None, axis...  8.27 us
    dynamic_slice x8, local copies, waits for them, and re-layouts, neighbour(): return lax.map(one_view, (queries, keys_wide, values_wide))  8.21 us
    reshape x1, local copies, waits for them, and re-layouts, body(): lax.all_gather(key_time, 'view', axis=0, tiled=True)  5.86 us
  transfers between devices with their start and end apart: 6, of which 6 were waited for; matrix products, arithmetic and copies ran while one was open for 13% of the time, Pallas kernels for 0%

commit v1 on v0

--- a/solution.py
+++ b/solution.py
@@ -8,6 +8,11 @@
 RADIUS = 3
 epsilon = 1e-06
 very_negative = -1e30
+
+
+def swapped_in(shard, mesh_axis, dim):
+    sent = jnp.stack([shard] * lax.axis_size(mesh_axis))
+    return jnp.concatenate(lax.all_to_all(sent, mesh_axis, 0, 0), axis=dim)
 
 
 def padded(block, sides, width):
@@ -130,7 +135,7 @@
         -1, positions, HEADS, HEAD_DIM
     )
     value_heads = (
-        lax.all_gather(value_time, "view", axis=0, tiled=True)
+        swapped_in(value_time, "view", 0)
         .reshape(-1, positions, HEADS, HEAD_DIM)
         .astype(jnp.float32)
     )

time: 167 us -> 160 us (0.958)
  the two profiles are of different devices: /device:TPU:1 before, /device:TPU:102 now
where the time goes in v1:
time: 160 us; the launch traced here: 159 us
  waiting for transfers between devices  49.7 us (31%)
  local copies, waits for them, and re-layouts  36 us (22%)
  matrix products  31.4 us (20%)
  starting transfers between devices  17 us (11%)
  between operations  13.7 us (9%)
  other arithmetic  10.8 us (7%)
    all_to_all x1, waiting for transfers between devices, swapped_in(): return jnp.concatenate(lax.all_to_all(sent, mesh_axis, 0, 0), axis=dim)  24.9 us
    ppermute x2, waiting for transfers between devices, padded(): lax.ppermute(lax.slice_in_dim(block, block.shape[dim] - width, None, axis...  14.3 us
    dot_general x8, matrix products, project(): result = jnp.dot(flat, weight_matrix, preferred_element_type=jnp.float32)  13.6 us
    ppermute x2, waiting for transfers between devices, padded(): lax.ppermute(lax.slice_in_dim(block, 0, width, axis=dim), axis, backward)  10.5 us
    ppermute x2, starting transfers between devices, padded(): lax.ppermute(lax.slice_in_dim(block, block.shape[dim] - width, None, axis...  8.42 us
    dynamic_slice x8, local copies, waits for them, and re-layouts, neighbour(): return lax.map(one_view, (queries, keys_wide, values_wide))  8.21 us
    reshape x1, local copies, waits for them, and re-layouts, body(): lax.all_gather(key_time, 'view', axis=0, tiled=True)  6 us
    dot_general x1, matrix products, body(): new_acc = jnp.einsum('qkph,kphe->qphe', weights, value_heads)  5.5 us
  transfers between devices with their start and end apart: 6, of which 5 were waited for; matrix products, arithmetic and copies ran while one was open for 10% of the time, Pallas kernels for 0%

profile of v1, /device:TPU:102, one launch (start us, length us, event | category | flops | bytes accessed | tf_op | source)
XLA Modules:
  0.0 158.8 jit_solution(7740678959094711113)
XLA Ops:
  6.6 1.3 fusion.40
  7.9 1.9 %fusion.28 = bf16[1,4,4,16,768]{4,3,2,1,0:T(8,128)(2,1)S(1)} fusion(bf16[768,768]{1,0:T(8,128)(2,1)} %param.16, bf16[4,4,16,768]{3,2,1,0:T(8,128)(2,1)} %param.13, f32[768]{0:T(1024)} %param.14, f32[4,4,16]{2,1,0:T(4,128)S(1)} %add_rsqrt_fusion.1), kind=kOutput, calls=%fused_computation.46 | convolution fusion | flops 302972928 | bytes 1970176 | tf_op jit(solution)/shard_map/dot_general | solution.py:39
  10.4 1.1 fusion.45
  11.5 5.0 %collective-permute-start = (bf16[2,4,3,16,768]{4,3,2,1,0:T(8,128)(2,1)}, bf16[2,4,3,16,768]{4,3,2,1,0:T(8,128)(2,1)S(1)}, u32[]{:S(2)}, u32[]{:S(2)}) collective-permute-start(bf16[2,4,3,16,768]{4,3,2,1,0:T(8,128)(2,1)} %get-tuple-element.103), channel_id=1, source_target_pairs={{0,8},{8,16},{16,24},{24,32},{32,40},{40,48},{48,56},{1,9},{9,17},... | collective-permute-start | bytes 1769480 | tf_op jit(solution)/shard_map/ppermute | solution.py:23
  16.5 1.9 %collective-permute-start.1 = (bf16[2,4,3,16,768]{4,3,2,1,0:T(8,128)(2,1)}, bf16[2,4,3,16,768]{4,3,2,1,0:T(8,128)(2,1)S(1)}, u32[]{:S(2)}, u32[]{:S(2)}) collective-permute-start(bf16[2,4,3,16,768]{4,3,2,1,0:T(8,128)(2,1)} %get-tuple-element.104), channel_id=1, source_target_pairs={{8,0},{16,8},{24,16},{32,24},{40,32},{48,40},{56,48},{9,1},{17,9},... | collective-permute-start | bytes 1769480 | tf_op jit(solution)/shard_map/ppermute | solution.py:26
  19.2 10.2 %collective-permute-done = bf16[2,4,3,16,768]{4,3,2,1,0:T(8,128)(2,1)S(1)} collective-permute-done((bf16[2,4,3,16,768]{4,3,2,1,0:T(8,128)(2,1)}, bf16[2,4,3,16,768]{4,3,2,1,0:T(8,128)(2,1)S(1)}, u32[]{:S(2)}, u32[]{:S(2)}) %collective-permute-start) | collective-permute-done | bytes 589856 | tf_op jit(solution)/shard_map/ppermute | solution.py:23
  29.4 5.2 %collective-permute-done.1 = bf16[2,4,3,16,768]{4,3,2,1,0:T(8,128)(2,1)S(1)} collective-permute-done((bf16[2,4,3,16,768]{4,3,2,1,0:T(8,128)(2,1)}, bf16[2,4,3,16,768]{4,3,2,1,0:T(8,128)(2,1)S(1)}, u32[]{:S(2)}, u32[]{:S(2)}) %collective-permute-start.1) | collective-permute-done | bytes 589856 | tf_op jit(solution)/shard_map/ppermute | solution.py:26
  34.6 1.3 pad_maximum_fusion.5
  36.0 3.4 %collective-permute-start.2 = (bf16[2,4,10,3,768]{4,3,2,1,0:T(4,128)(2,1)}, bf16[2,4,10,3,768]{4,3,2,1,0:T(4,128)(2,1)}, u32[]{:S(2)}, u32[]{:S(2)}) collective-permute-start(bf16[2,4,10,3,768]{4,3,2,1,0:T(4,128)(2,1)} %get-tuple-element.101), channel_id=1, source_target_pairs={{0,1},{1,2},{2,3},{3,4},{4,5},{5,6},{6,7},{8,9},{9,10},{10,11},{11... | collective-permute-start | bytes 1105928 | tf_op jit(solution)/shard_map/ppermute | solution.py:23
  39.4 2.4 %collective-permute-start.3 = (bf16[2,4,10,3,768]{4,3,2,1,0:T(4,128)(2,1)}, bf16[2,4,10,3,768]{4,3,2,1,0:T(4,128)(2,1)}, u32[]{:S(2)}, u32[]{:S(2)}) collective-permute-start(bf16[2,4,10,3,768]{4,3,2,1,0:T(4,128)(2,1)} %get-tuple-element.102), channel_id=1, source_target_pairs={{1,0},{2,1},{3,2},{4,3},{5,4},{6,5},{7,6},{9,8},{10,9},{11,10},{12... | collective-permute-start | bytes 1105928 | tf_op jit(solution)/shard_map/ppermute | solution.py:26
  42.6 0.7 sub.85
  43.3 2.6 %convolution_convert_fusion.4 = bf16[4,4,16,768]{3,2,1,0:T(8,128)(2,1)} fusion(bf16[768,768]{1,0:T(8,128)(2,1)} %param.15, bf16[4,4,16,768]{3,2,1,0:T(8,128)(2,1)S(1)} %copy-done.2, f32[768]{0:T(1024)} %param.14, f32[4,4,16]{2,1,0:T(4,128)} %copy-done.6), kind=kOutput, calls=%fused_computation.43 | convolution fusion | flops 302972928 | bytes 1970176 | tf_op jit(solution)/shard_map/dot_general | solution.py:39
  45.9 4.1 %collective-permute-done.2 = bf16[2,4,10,3,768]{4,3,2,1,0:T(4,128)(2,1)} collective-permute-done((bf16[2,4,10,3,768]{4,3,2,1,0:T(4,128)(2,1)}, bf16[2,4,10,3,768]{4,3,2,1,0:T(4,128)(2,1)}, u32[]{:S(2)}, u32[]{:S(2)}) %collective-permute-start.2) | collective-permute-done | bytes 368672 | tf_op jit(solution)/shard_map/ppermute | solution.py:23
  50.0 5.2 %collective-permute-done.3 = bf16[2,4,10,3,768]{4,3,2,1,0:T(4,128)(2,1)} collective-permute-done((bf16[2,4,10,3,768]{4,3,2,1,0:T(4,128)(2,1)}, bf16[2,4,10,3,768]{4,3,2,1,0:T(4,128)(2,1)}, u32[]{:S(2)}, u32[]{:S(2)}) %collective-permute-start.3) | collective-permute-done | bytes 368672 | tf_op jit(solution)/shard_map/ppermute | solution.py:26
  55.2 3.1 %pad_maximum_fusion = bf16[2,4,10,22,768]{4,3,2,1,0:T(8,128)(2,1)S(1)} fusion(bf16[2,4,10,3,768]{4,3,2,1,0:T(4,128)(2,1)} %collective-permute-done.3, bf16[2,4,3,16,768]{4,3,2,1,0:T(8,128)(2,1)S(1)} %collective-permute-done.1, bf16[1,4,4,16,768]{4,3,2,1,0:T(8,128)(2,1)S(1)} %fusion.29, bf16[1,4,4,16,768]{4,3,2,1,0:T(8,128)(2,1)S(1)} %fusion.28, ...), kind=kLoop, calls=%fused_computation.26 | loop fusion | flops 16220160 | bytes 5406720 | tf_op jit(solution)/shard_map/concatenate | solution.py:27
  58.4 1.8 %slice_bitcast_fusion = (bf16[4,10,22,768]{3,2,1,0:T(8,128)(2,1)}, bf16[4,10,22,768]{3,2,1,0:T(8,128)(2,1)}) fusion(bf16[2,4,10,22,768]{4,3,2,1,0:T(8,128)(2,1)S(1)} %pad_maximum_fusion), kind=kLoop, calls=%fused_computation.33 | loop fusion | bytes 5406720 | tf_op jit(solution)/shard_map/squeeze | solution.py:118
  60.2 26.6 %while.11 = (s32[]{:T(128)}, bf16[4,4,16,768]{3,2,1,0:T(8,128)(2,1)}, bf16[4,10,22,768]{3,2,1,0:T(8,128)(2,1)}, bf16[4,4,16,768]{3,2,1,0:T(8,128)(2,1)}, bf16[4,...) while((s32[]{:T(128)}, ...), condition=%wide.region_4.5_spmd.clone, body=%wide.region_1.4_spmd.clone.sunk | while | flops 152731136 | bytes 6633009 | solution.py:91
  60.2 1.1 constant_dynamic-slice_fusion.5
  62.0 0.9 constant_dynamic-slice_fusion.6
  64.6 1.2 fusion.73
  66.2 0.7 constant_dynamic-update-slice_fusion.2
  66.8 1.1 constant_dynamic-slice_fusion.5
  68.6 0.9 constant_dynamic-slice_fusion.6
  71.2 1.2 fusion.73
  72.8 0.7 constant_dynamic-update-slice_fusion.2
  73.5 1.1 constant_dynamic-slice_fusion.5
  75.3 0.9 constant_dynamic-slice_fusion.6
  76.4 0.6 fusion.71
  77.9 1.2 fusion.73
  79.5 0.7 constant_dynamic-update-slice_fusion.2
  80.2 1.1 constant_dynamic-slice_fusion.5
  82.0 0.9 constant_dynamic-slice_fusion.6
  83.0 0.6 fusion.71
  84.6 1.2 fusion.73
  86.2 0.7 constant_dynamic-update-slice_fusion.2
  86.8 1.8 %multiply_reduce_fusion = (f32[4,4,16]{2,1,0:T(4,128)S(1)}, f32[4,4,16,768]{3,2,1,0:T(8,128)S(1)}) fusion(bf16[4,4,16,768]{3,2,1,0:T(8,128)(2,1)} %get-tuple-element.37, bf16[768,768]{1,0:T(8,128)(2,1)S(1)} %copy-done, bf16[4,4,16,768]{3,2,1,0:T(8,128)(2,1)} %param.13), kind=kOutput, calls=%fused_computation.67 | convolution fusion | flops 303169280 | bytes 2753536 | tf_op jit(solution)/shard_map/dot_general | solution.py:39
  88.8 1.2 convolution_convert_fusion.2
  90.7 1.3 stack.19
  92.0 4.2 %all-to-all-start = ((bf16[4,4,4,16,768]{4,3,2,1,0:T(8,128)(2,1)}), bf16[4,4,4,16,768]{4,3,2,1,0:T(8,128)(2,1)S(1)}, u32[]{:S(2)}, u32[]{:S(2)}) async-start(bf16[4,4,4,16,768]{4,3,2,1,0:T(8,128)(2,1)} %stack.19), calls=%async_computation | async-start | bytes 3145728 | tf_op jit(solution)/shard_map/all_to_all | solution.py:15
  96.2 2.6 %convolution_convert_fusion.1 = bf16[4,4,16,768]{3,2,1,0:T(8,128)(2,1)} fusion(bf16[4,4,16,768]{3,2,1,0:T(8,128)(2,1)} %copy-done.4, bf16[768,768]{1,0:T(8,128)(2,1)} %param.20), kind=kOutput, calls=%fused_computation.40 | convolution fusion | flops 302186496 | bytes 1966080 | tf_op jit(solution)/shard_map/dot_general | solution.py:39
  98.8 2.4 %reshape.288 = bf16[4,64,12,64]{3,2,1,0:T(8,128)(2,1)} reshape(bf16[4,4,16,768]{3,2,1,0:T(8,128)(2,1)} %convolution_convert_fusion.1) | data formatting | bytes 786432 | tf_op jit(solution)/shard_map/reshape | solution.py:132
  101.2 24.9 %all-to-all-done = bf16[4,4,4,16,768]{4,3,2,1,0:T(8,128)(2,1)S(1)} async-done(((bf16[4,4,4,16,768]{4,3,2,1,0:T(8,128)(2,1)}), bf16[4,4,4,16,768]{4,3,2,1,0:T(8,128)(2,1)S(1)}, u32[]{:S(2)}, u32[]{:S(2)}) %all-to-all-start) | async-done | bytes 1572896 | tf_op jit(solution)/shard_map/all_to_all | solution.py:15
  126.2 3.8 %reshape_reshape.3 = bf16[16,64,12,64]{3,2,1,0:T(8,128)(2,1)} reshape(bf16[4,4,4,16,768]{4,3,2,1,0:T(8,128)(2,1)S(1)} %all-to-all-done) | data formatting | bytes 3145728 | tf_op jit(solution)/shard_map/reshape;reshape | solution.py:139
  130.0 6.0 %reshape.287 = bf16[16,64,12,64]{3,2,1,0:T(8,128)(2,1)} reshape(bf16[16,4,16,768]{3,2,1,0:T(8,128)(2,1)} %all-gather.2.cloned.1.call-done) | data formatting | bytes 3145728 | tf_op jit(solution)/shard_map/reshape | solution.py:134
  136.0 5.1 %bitcast_reduce_fusion = (f32[4,64,12]{0,2,1:T(8,128)S(1)}, f32[64,12,16,4]{2,3,1,0:T(4,128)S(1)}) fusion(bf16[4,64,12,64]{3,2,1,0:T(8,128)(2,1)S(1)} %copy-done.3, bf16[16,64,12,64]{3,2,1,0:T(8,128)(2,1)} %reshape.287), kind=kOutput, calls=%fused_computation.29 | convolution fusion | flops 6386688 | bytes 2174976 | tf_op jit(solution)/shard_map/qphe,kphe->qkph/dot_general | solution.py:143
  141.2 1.9 %fusion.30 = f32[4,64,12]{0,2,1:T(8,128)S(1)} fusion(f32[64,12,16,4]{2,3,1,0:T(4,128)S(1)} %get-tuple-element.108, f32[4,64,12]{0,2,1:T(8,128)S(1)} %broadcast_maximum_fusion), kind=kLoop, calls=%fused_computation.48 | loop fusion | flops 95232 | bytes 221184 | tf_op jit(solution)/shard_map/reduce_sum | solution.py:148
  143.1 5.5 %fusion.19 = bf16[4,64,12,64]{3,0,2,1:T(4,128)(2,1)S(1)} fusion(bf16[16,64,12,64]{3,2,1,0:T(8,128)(2,1)S(1)} %copy-done.1, f32[64,12,16,4]{2,3,1,0:T(4,128)S(1)} %get-tuple-element.108, f32[4,64,12]{0,2,1:T(8,128)S(1)} %fusion.30, f32[4,64,12]{0,2,1:T(8,128)S(1)} %broadcast_maximum_fusion), kind=kOutput, calls=%fused_computation.31 | convolution fusion | flops 6733824 | bytes 2187264 | tf_op jit(solution)/shard_map/qkph,kphe->qphe/dot_general | solution.py:149
  149.5 2.5 %fusion.27 = bf16[4,4,16,768]{3,2,1,0:T(8,128)(2,1)} fusion(f32[4,4,16,768]{3,2,1,0:T(8,128)S(1)} %get-tuple-element.106, bf16[4,4,16,768]{3,2,1,0:T(8,128)(2,1)S(1)} %convert_element_type.76, bf16[768,768]{1,0:T(8,128)(2,1)} %param.23), kind=kOutput, calls=%fused_computation.39 | convolution fusion | flops 302383104 | bytes 2752512 | tf_op jit(solution)/shard_map/dot_general | solution.py:39
  (75 shorter events, 13.4 us)
Async XLA Ops:
  6.5 80.3 %copy-start = (bf16[768,768]{1,0:T(8,128)(2,1)S(1)}, bf16[768,768]{1,0:T(8,128)(2,1)}, u32[]{:S(2)}) copy-start(bf16[768,768]{1,0:T(8,128)(2,1)} %param.18) | copy-start | bytes 3538948
  6.5 3.3 %copy-start.2 = (bf16[4,4,16,768]{3,2,1,0:T(8,128)(2,1)S(1)}, bf16[4,4,16,768]{3,2,1,0:T(8,128)(2,1)}, u32[]{:S(2)}) copy-start(bf16[4,4,16,768]{3,2,1,0:T(8,128)(2,1)} %param.13) | copy-start | bytes 1179652
  6.5 3.3 %copy-start.11 = (f32[768]{0:T(1024)S(1)}, f32[768]{0:T(1024)}, u32[]{:S(2)}) copy-start(f32[768]{0:T(1024)} %param.14) | copy-start | bytes 9220
  6.5 123.5 %all-gather.2.cloned.1.call-start = ((), (), s32[]{:S(2)}) async-start(), calls=%async_computation.1 | async-start | bytes 1966080 | tf_op jit(solution)/shard_map/all_gather | solution.py:134
  6.5 3.3 %copy-start.8 = (bf16[768,768]{1,0:T(8,128)(2,1)S(1)}, bf16[768,768]{1,0:T(8,128)(2,1)}, u32[]{:S(2)}) copy-start(bf16[768,768]{1,0:T(8,128)(2,1)} %param.17) | copy-start | bytes 3538948
  7.9 2.5 %copy-start.6 = (f32[4,4,16]{2,1,0:T(4,128)}, f32[4,4,16]{2,1,0:T(4,128)S(1)}, u32[]{:S(2)}) copy-start(f32[4,4,16]{2,1,0:T(4,128)S(1)} %add_rsqrt_fusion.1) | copy-start | bytes 3076
  11.5 17.9 %collective-permute-start = (bf16[2,4,3,16,768]{4,3,2,1,0:T(8,128)(2,1)}, bf16[2,4,3,16,768]{4,3,2,1,0:T(8,128)(2,1)S(1)}, u32[]{:S(2)}, u32[]{:S(2)}) collective-permute-start(bf16[2,4,3,16,768]{4,3,2,1,0:T(8,128)(2,1)} %get-tuple-element.103), channel_id=1, source_target_pairs={{0,8},{8,16},{16,24},{24,32},{32,40},{40,48},{48,56},{1,9},{9,17},... | collective-permute-start | bytes 1769480 | tf_op jit(solution)/shard_map/ppermute | solution.py:23
  16.5 18.1 %collective-permute-start.1 = (bf16[2,4,3,16,768]{4,3,2,1,0:T(8,128)(2,1)}, bf16[2,4,3,16,768]{4,3,2,1,0:T(8,128)(2,1)S(1)}, u32[]{:S(2)}, u32[]{:S(2)}) collective-permute-start(bf16[2,4,3,16,768]{4,3,2,1,0:T(8,128)(2,1)} %get-tuple-element.104), channel_id=1, source_target_pairs={{8,0},{16,8},{24,16},{32,24},{40,32},{48,40},{56,48},{9,1},{17,9},... | collective-permute-start | bytes 1769480 | tf_op jit(solution)/shard_map/ppermute | solution.py:26
  36.0 14.0 %collective-permute-start.2 = (bf16[2,4,10,3,768]{4,3,2,1,0:T(4,128)(2,1)}, bf16[2,4,10,3,768]{4,3,2,1,0:T(4,128)(2,1)}, u32[]{:S(2)}, u32[]{:S(2)}) collective-permute-start(bf16[2,4,10,3,768]{4,3,2,1,0:T(4,128)(2,1)} %get-tuple-element.101), channel_id=1, source_target_pairs={{0,1},{1,2},{2,3},{3,4},{4,5},{5,6},{6,7},{8,9},{9,10},{10,11},{11... | collective-permute-start | bytes 1105928 | tf_op jit(solution)/shard_map/ppermute | solution.py:23
  39.4 15.9 %collective-permute-start.3 = (bf16[2,4,10,3,768]{4,3,2,1,0:T(4,128)(2,1)}, bf16[2,4,10,3,768]{4,3,2,1,0:T(4,128)(2,1)}, u32[]{:S(2)}, u32[]{:S(2)}) collective-permute-start(bf16[2,4,10,3,768]{4,3,2,1,0:T(4,128)(2,1)} %get-tuple-element.102), channel_id=1, source_target_pairs={{1,0},{2,1},{3,2},{4,3},{5,4},{6,5},{7,6},{9,8},{10,9},{11,10},{12... | collective-permute-start | bytes 1105928 | tf_op jit(solution)/shard_map/ppermute | solution.py:26
  58.4 1.8 %copy-start.5 = (pred[220]{0:T(512)(128)(4,1)S(1)}, pred[220]{0:T(512)(128)(4,1)}, u32[]{:S(2)}) copy-start(pred[220]{0:T(512)(128)(4,1)} %reshape.289) | copy-start | bytes 664
  86.8 1.8 %copy-start.7 = (f32[768]{0:T(1024)S(1)}, f32[768]{0:T(1024)}, u32[]{:S(2)}) copy-start(f32[768]{0:T(1024)} %param.19) | copy-start | bytes 9220
  86.8 1.9 %copy-start.9 = (bf16[768,768]{1,0:T(8,128)(2,1)S(1)}, bf16[768,768]{1,0:T(8,128)(2,1)}, u32[]{:S(2)}) copy-start(bf16[768,768]{1,0:T(8,128)(2,1)} %param.21) | copy-start | bytes 3538948
  88.8 1.9 %copy-start.4 = (bf16[4,4,16,768]{3,2,1,0:T(8,128)(2,1)}, bf16[4,4,16,768]{3,2,1,0:T(8,128)(2,1)S(1)}, u32[]{:S(2)}) copy-start(bf16[4,4,16,768]{3,2,1,0:T(8,128)(2,1)S(1)} %multiply_convert_fusion) | copy-start | bytes 1179652
  88.8 1.4 copy-start.10
  92.0 34.2 %all-to-all-start = ((bf16[4,4,4,16,768]{4,3,2,1,0:T(8,128)(2,1)}), bf16[4,4,4,16,768]{4,3,2,1,0:T(8,128)(2,1)S(1)}, u32[]{:S(2)}, u32[]{:S(2)}) async-start(bf16[4,4,4,16,768]{4,3,2,1,0:T(8,128)(2,1)} %stack.19), calls=%async_computation | async-start | bytes 3145728 | tf_op jit(solution)/shard_map/all_to_all | solution.py:15
  130.0 6.0 %copy-start.3 = (bf16[4,64,12,64]{3,2,1,0:T(8,128)(2,1)S(1)}, bf16[4,64,12,64]{3,2,1,0:T(8,128)(2,1)}, u32[]{:S(2)}) copy-start(bf16[4,64,12,64]{3,2,1,0:T(8,128)(2,1)} %reshape.288) | copy-start | bytes 1179652
  136.0 7.1 %copy-start.1 = (bf16[16,64,12,64]{3,2,1,0:T(8,128)(2,1)S(1)}, bf16[16,64,12,64]{3,2,1,0:T(8,128)(2,1)}, u32[]{:S(2)}) copy-start(bf16[16,64,12,64]{3,2,1,0:T(8,128)(2,1)} %reshape_reshape.3) | copy-start | bytes 4718596
Sparse Core Ops, SparseCore 0:
  90.2 33.4 all-gather.1
